TPU v7x, 32 devices: a whole 2x2x4 slice. The times are simulated.
32 devices in a mesh: beam: 4 (over z), pulse: 4 (over x, core), range: 2 (over y).
Axes of the slice: x: 2, y: 2, z: 4, core: 2. Of those that a mesh axis runs over, the one named last changes fastest.
Arguments:
- signal: bfloat16 [8, 32, 2, 1024], P('beam', 'pulse', None, 'range'), may hold values from -40 to 40, as said below
- replica: bfloat16 [2, 2048], P(None, ('beam', 'pulse')), may hold values from -0.09375 to 0.09375
- guard_cells: int32 [8], P('beam'), may hold values from 1 to 8, as said below
- train_cells: int32 [8], P('beam'), may hold values from 64 to 96, as said below
- scale_index: int32 [8], P('beam'), may hold values from 0 to 15
- offsets: int32 [8], P('beam'), may hold values from 0 to 127, as said below
Outputs:
- compressed: bfloat16 [8, 32, 2, 1024], P('beam', 'pulse', None, 'range')
- test_ratio: float32 [8, 32, 1024], P('beam', 'pulse', 'range')
Inputs may be any that keep to these rules, and one draw needn't show every extreme that they name: `signal`: values stay within the range, with cell-to-cell varying levels. `guard_cells`: some beam has exactly 8 guard cells. `train_cells`: the beam with 8 guard cells has 96 training cells. `offsets`: some beam has the offset 128 - 1.
All inputs are finite; a program needn't handle non-finite values.
Results may differ from a plain program's by a relative error of at most 0.001.
Values may be sent and summed in bfloat16 or wider, within the bound.
A program may use at most 64 MiB of HBM per device.

v0:
```python
import jax
import jax.numpy as jnp
from jax import lax
from jax.sharding import PartitionSpec as P

TILE = 128
OFF_MAX = 128
GUARD_MAX = 8
TRAIN_MAX = 96
EPSILON = 1e-06


def passed_along(array, axis, by):
    devices = lax.axis_size(axis)
    pairs = [(i, i + by) for i in range(devices) if 0 <= i + by < devices]
    return lax.ppermute(array, axis, pairs)


def padded_2(cells, sides, width):
    for axis, dim in sides:
        count = lax.axis_size(axis)
        ends = count - 1
        head = lax.slice_in_dim(cells, 0, width, axis=dim)
        tail = lax.slice_in_dim(cells, cells.shape[dim] - width, cells.shape[dim], axis=dim)
        cells = jnp.concatenate(
            [
                lax.ppermute(tail, axis, [(i, (i + 1) % count) for i in range(ends)]),
                cells,
                lax.ppermute(head, axis, [((i + 1) % count, i) for i in range(ends)]),
            ],
            axis=dim,
        )
    return cells


def panels(whole):
    width = TILE + whole.shape[1]

    def skewed(values):
        padded = jnp.concatenate([values, jnp.zeros((TILE + 1,), values.dtype)])
        flat = jnp.tile(padded, TILE)[: TILE * width]
        return flat.reshape(TILE, width)

    return (skewed(whole[0]), skewed(whole[1]))


def compress(extended, offsets, panel_real, panel_imag, tiles):
    beams, pulses = (extended.shape[0], extended.shape[1])
    width = panel_real.shape[1]
    span = tiles * TILE + width - TILE

    def align(block, start):
        return lax.dynamic_slice_in_dim(block, start, span, 2)

    aligned = jax.vmap(align)(extended, offsets)
    rows = beams * pulses
    group = max(1, min(tiles, 256 // rows))
    while tiles % group:
        group = group - 1
    blocks = tiles // group
    dims = (((1,), (1,)), ((), ()))

    def block_fn(index):
        first = index * (group * TILE)
        windows = jnp.stack(
            [
                lax.dynamic_slice_in_dim(aligned, first + step * TILE, width, 3)
                for step in range(group)
            ]
        )
        real_part = windows[:, :, :, 0, :].reshape(group * rows, width)
        imag_part = windows[:, :, :, 1, :].reshape(group * rows, width)
        out_real = lax.dot_general(
            real_part, panel_real, dims, preferred_element_type=jnp.float32
        ) + lax.dot_general(imag_part, panel_imag, dims, preferred_element_type=jnp.float32)
        out_imag = lax.dot_general(
            imag_part, panel_real, dims, preferred_element_type=jnp.float32
        ) - lax.dot_general(real_part, panel_imag, dims, preferred_element_type=jnp.float32)
        return jnp.stack([out_real, out_imag], axis=1).reshape(group, beams, pulses, 2, TILE)

    outputs = lax.map(block_fn, jnp.arange(blocks, dtype=jnp.int32))
    outputs = outputs.reshape(tiles, beams, pulses, 2, TILE)
    return jnp.transpose(outputs, (1, 2, 3, 0, 4)).reshape(beams, pulses, 2, tiles * TILE)


def cell_power(compressed):
    real_part = compressed[:, :, 0].astype(jnp.float32)
    imag_part = compressed[:, :, 1].astype(jnp.float32)
    return real_part * real_part + imag_part * imag_part


def detect(padded, guard_cells, train_cells, scale_index, first_gate, total_gates):
    margin = GUARD_MAX + TRAIN_MAX
    beams, pulses = (padded.shape[0], padded.shape[1])
    length = padded.shape[2] - 2 * margin
    running = jnp.cumsum(padded, axis=2)
    prefix = jnp.concatenate([jnp.zeros((beams, pulses, 1), jnp.float32), running], axis=2)
    local = jnp.arange(length, dtype=jnp.int32)[None, :]
    guard = guard_cells[:, None]
    train = train_cells[:, None]

    def window(block, start):
        return lax.dynamic_slice_in_dim(block, start, length, 1)

    def pick(starts):
        return jax.vmap(window)(prefix, starts)

    lag = pick(margin - guard_cells) - pick(margin - guard_cells - train_cells)
    lead = pick(margin + guard_cells + train_cells + 1) - pick(margin + guard_cells + 1)
    position = first_gate + local
    count = jnp.clip(position - guard, 0, train) + jnp.clip(
        total_gates - 1 - position - guard, 0, train
    )
    noise = (lag + lead) / count.astype(jnp.float32)[:, None, :]
    factor = jnp.exp2(scale_index.astype(jnp.float32) / 8.0)
    power = padded[:, :, margin : margin + length]
    return power / (factor[:, None, None] * (noise + EPSILON))


def body(signal, replica, guard_cells, train_cells, scale_index, offsets):
    whole = lax.all_gather(replica, ("beam", "pulse"), axis=1, tiled=True)
    panel_real, panel_imag = panels(whole)
    gate_count = signal.shape[3]
    margin = GUARD_MAX + TRAIN_MAX
    needed = whole.shape[1] + OFF_MAX
    limit = min(-(-needed // gate_count), lax.axis_size("range") - 1)
    pieces = [signal]
    for step in range(1, limit + 1):
        keep = min(gate_count, needed - (step - 1) * gate_count)
        pieces.append(passed_along(signal[:, :, :, :keep], "range", -step))
    extended = jnp.concatenate(pieces, axis=3)
    extra = gate_count + needed - extended.shape[3]
    extended = jnp.pad(extended, ((0, 0), (0, 0), (0, 0), (0, extra)))
    compressed = compress(extended, offsets, panel_real, panel_imag, gate_count // TILE).astype(
        jnp.bfloat16
    )
    power = cell_power(compressed)
    padded = padded_2(power, (("range", 2),), margin)
    first_gate = lax.axis_index("range") * gate_count
    total_gates = gate_count * lax.axis_size("range")
    test_ratio = detect(padded, guard_cells, train_cells, scale_index, first_gate, total_gates)
    return (compressed, test_ratio)


def solution(mesh):
    placed = (
        P("beam", "pulse", None, "range"),
        P(None, ("beam", "pulse")),
        P("beam"),
        P("beam"),
        P("beam"),
        P("beam"),
    )
    return jax.shard_map(
        body,
        mesh=mesh,
        in_specs=placed,
        out_specs=(P("beam", "pulse", None, "range"), P("beam", "pulse", "range")),
        check_vma=False,
    )
```

profile of v0, /device:TPU:0, one launch (start us, length us, event | category | flops | bytes accessed | tf_op | source)
XLA Modules:
  0.0 62.5 jit_solution(7068981721563648878)
XLA Ops:
  0.6 1.3 %collective-permute-start = (bf16[2,8,2,512]{3,2,1,0:T(2,128)(2,1)}, bf16[2,8,2,512]{3,2,1,0:T(2,128)(2,1)S(1)}, u32[]{:S(2)}, u32[]{:S(2)}) collective-permute-start(bf16[2,8,2,512]{3,2,1,0:T(2,128)(2,1)} %param.6), channel_id=1, source_target_pairs={{1,0},{3,2},{5,4},{7,6},{9,8},{11,10},{13,12},{15,14},{17,16},{19,... | collective-permute-start | bytes 98312 | tf_op jit(solution)/shard_map/ppermute | solution.py:16
  1.9 0.0 copy-start.4
  1.9 0.6 %copy-done.4 = s32[2]{0:T(128)S(1)} copy-done((s32[2]{0:T(128)S(1)}, s32[2]{0:T(128)}, u32[]{:S(2)}) %copy-start.4) | copy-done | bytes 32
  2.6 0.0 copy-start.3
  2.6 0.6 %copy-done.3 = bf16[2,128]{1,0:T(2,128)(2,1)S(1)} copy-done((bf16[2,128]{1,0:T(2,128)(2,1)S(1)}, bf16[2,128]{1,0:T(2,128)(2,1)}, u32[]{:S(2)}) %copy-start.3) | copy-done | bytes 536
  3.2 23.1 %all_gather.3 = bf16[2,2048]{1,0:T(2,128)(2,1)S(1)} all-gather(bf16[2,128]{1,0:T(2,128)(2,1)S(1)} %copy-done.3), channel_id=1, replica_groups=mesh['beam'=4,'pulse'=4,'range'=2] {'beam','pulse'}, dimensions={1}, use_global_device_ids=true | all-gather | bytes 8704 | tf_op jit(solution)/shard_map/all_gather | solution.py:121
  26.3 0.0 copy-start.1
  26.3 0.0 copy-start.2
  26.3 0.1 slice_reduce_fusion
  26.4 0.6 copy-done.1
  27.0 0.0 copy-done.2
  27.0 0.1 add_convert_fusion
  27.1 0.1 copy.41
  27.3 0.7 %tile.9 = bf16[278656]{0:T(1024)(128)(2,1)S(1)} reshape(bf16[128,2177]{1,0:T(8,128)(2,1)S(1)} %tile.8) | data formatting | bytes 1114624 | tf_op jit(solution)/shard_map/tile | solution.py:41
  28.0 0.6 reshape.119
  28.7 0.7 %tile.21 = bf16[278656]{0:T(1024)(128)(2,1)S(1)} reshape(bf16[128,2177]{1,0:T(8,128)(2,1)S(1)} %tile.20) | data formatting | bytes 1114624 | tf_op jit(solution)/shard_map/tile | solution.py:41
  29.5 0.0 copy-start
  29.5 0.6 reshape.120
  30.1 0.0 collective-permute-done
  30.1 0.1 copy-done
  30.3 0.1 fusion.4
  30.4 4.0 %while.1 = (s32[]{:T(128)}, bf16[2,8,2,2688]{3,2,1,0:T(2,128)(2,1)S(1)}, s32[2,4]{1,0:T(2,128)S(1)}, bf16[2,8,2,2560]{3,1,0,2:T(8,128)(2,1)S(1)}, s32[]{:T(128)}) while((s32[]{:T(128)}, bf16[2,8,2,2688]{3,2,1,0:T(2,128)(2,1)S(1)}, s32[2,4]{1,0:T(2,128)S(1)}, bf16[2,8,2,2560]{3,1,0,2:T(8,128)(2,1)S(1)}, s32[]{:T(128)}) %tuple.43), condition=%wide.while_cond, body=%wide.while_body.sunk | while | flops 2 | bytes 327813 | solution.py:53
  30.4 0.6 fusion.34
  31.0 1.4 %constant_dynamic-slice_fusion.5 = bf16[1,8,2,2560]{3,2,1,0:T(2,128)(2,1)S(1)} fusion(bf16[2,8,2,2688]{3,2,1,0:T(2,128)(2,1)S(1)} %get-tuple-element.115, s32[]{:T(128)} %bitcast.68, s32[]{:T(128)} %bitcast.69), kind=kLoop, calls=%fused_computation.6.clone.1 | loop fusion | bytes 163848 | tf_op jit(solution)/shard_map/vmap()/gather
  32.4 0.6 fusion.34
  33.0 1.4 %constant_dynamic-slice_fusion.5 = bf16[1,8,2,2560]{3,2,1,0:T(2,128)(2,1)S(1)} fusion(bf16[2,8,2,2688]{3,2,1,0:T(2,128)(2,1)S(1)} %get-tuple-element.115, s32[]{:T(128)} %bitcast.68, s32[]{:T(128)} %bitcast.69), kind=kLoop, calls=%fused_computation.6.clone.1 | loop fusion | bytes 163848 | tf_op jit(solution)/shard_map/vmap()/gather
  34.4 0.1 pad_maximum_fusion
  34.6 0.3 fusion.24
  34.9 0.3 fusion.23
  35.2 0.3 fusion.1
  35.6 0.3 fusion
  35.9 0.1 fusion.22
  36.0 0.0 copy-start.5
  36.0 4.7 %collective-permute-start.1 = (f32[2,8,104]{2,1,0:T(8,128)S(1)}, f32[2,8,104]{2,1,0:T(8,128)S(1)}, u32[]{:S(2)}, u32[]{:S(2)}) collective-permute-start(f32[2,8,104]{2,1,0:T(8,128)S(1)} %get-tuple-element.67), channel_id=1, source_target_pairs={{0,1},{2,3},{4,5},{6,7},{8,9},{10,11},{12,13},{14,15},{16,17},{18,... | collective-permute-start | bytes 19976 | tf_op jit(solution)/shard_map/ppermute | solution.py:27
  40.7 1.5 %collective-permute-start.2 = (f32[2,8,104]{2,1,0:T(8,128)S(1)}, f32[2,8,104]{2,1,0:T(8,128)S(1)}, u32[]{:S(2)}, u32[]{:S(2)}) collective-permute-start(f32[2,8,104]{2,1,0:T(8,128)S(1)} %get-tuple-element.68), channel_id=1, source_target_pairs={{1,0},{3,2},{5,4},{7,6},{9,8},{11,10},{13,12},{15,14},{17,16},{19,... | collective-permute-start | bytes 19976 | tf_op jit(solution)/shard_map/ppermute | solution.py:29
  42.2 0.0 copy-done.5
  42.2 0.6 %copy.55 = bf16[2,8,2,512]{3,2,1,0:T(2,128)(2,1)} copy(bf16[2,8,2,512]{3,1,2,0:T(8,128)(2,1)S(1)} %copy_bitcast_fusion) | data formatting | bytes 65536
  42.8 0.0 collective-permute-done.1
  42.8 3.4 %collective-permute-done.2 = f32[2,8,104]{2,1,0:T(8,128)S(1)} collective-permute-done((f32[2,8,104]{2,1,0:T(8,128)S(1)}, f32[2,8,104]{2,1,0:T(8,128)S(1)}, u32[]{:S(2)}, u32[]{:S(2)}) %collective-permute-start.2) | collective-permute-done | bytes 6688 | tf_op jit(solution)/shard_map/ppermute | solution.py:29
  46.2 0.1 fusion.5
  46.3 3.4 %reduce-window.6 = f32[2,8,6,128]{3,1,2,0:T(8,128)S(1)} reduce-window(f32[2,8,6,128]{3,1,2,0:T(8,128)S(1)} %fusion.5, f32[]{:T(128)} %constant.72.clone.1), window={size=1x1x1x128 pad=0_0x0_0x0_0x127_0}, to_apply=%region_0.1 | reduce-window | flops 1560576 | bytes 98308 | tf_op jit(solution)/shard_map/reduce-window
  49.7 0.1 slice.106
  49.8 0.1 copy.48
  50.0 0.1 add_bitcast_fusion
  50.0 0.3 copy.59
  50.4 0.3 concatenate.37
  50.6 2.6 %gather_fusion.3 = f32[2,8,512]{1,0,2:T(2,128)S(1)} fusion(f32[2,8,721]{1,0,2:T(2,128)S(1)} %concatenate.37, s32[2]{0:T(128)S(1)} %get-tuple-element.72), kind=kCustom, calls=%fused_computation.3 | custom fusion | bytes 65560 | tf_op jit(solution)/shard_map/vmap()/gather | solution.py:103
  53.2 0.2 copy.54
  53.4 2.6 %gather_fusion.2 = f32[2,8,512]{1,0,2:T(2,128)S(1)} fusion(f32[2,8,721]{1,0,2:T(2,128)S(1)} %concatenate.37, s32[2]{0:T(128)S(1)} %get-tuple-element.70), kind=kCustom, calls=%fused_computation.2 | custom fusion | bytes 65560 | tf_op jit(solution)/shard_map/vmap()/gather | solution.py:103
  56.0 0.2 copy.53
  56.2 2.6 %gather_fusion.1 = f32[2,8,512]{1,0,2:T(2,128)S(1)} fusion(f32[2,8,721]{1,0,2:T(2,128)S(1)} %concatenate.37, s32[2]{0:T(128)S(1)} %get-tuple-element.69), kind=kCustom, calls=%fused_computation.1 | custom fusion | bytes 65560 | tf_op jit(solution)/shard_map/vmap()/gather | solution.py:103
  58.8 0.2 copy.52
  59.0 2.6 %gather_fusion = f32[2,8,512]{1,0,2:T(2,128)S(1)} fusion(f32[2,8,721]{1,0,2:T(2,128)S(1)} %concatenate.37, s32[2]{0:T(128)S(1)} %get-tuple-element.71), kind=kCustom, calls=%fused_computation | custom fusion | bytes 65560 | tf_op jit(solution)/shard_map/vmap()/gather | solution.py:103
  61.6 0.2 copy.51
  61.8 0.7 %multiply_divide_fusion = f32[2,8,512]{2,1,0:T(8,128)} fusion(f32[2,8,512]{2,1,0:T(8,128)S(1)} %copy.53, f32[2,8,512]{2,1,0:T(8,128)S(1)} %copy.54, f32[2,8,512]{2,1,0:T(8,128)S(1)} %copy.51, f32[2,8,512]{2,1,0:T(8,128)S(1)} %copy.52, f32[2,512]{1,0:T(2,128)S(1)} %add_convert_fusion, f32[2]{0:T(128)S(1)} %multiply_exponential_fusion, ...), kind=kLoop, calls=%fused_computation.27 | loop fusion | flops 98304 | bytes 200712 | tf_op jit(solution)/shard_map/div | solution.py:117
  (24 shorter events, 0.4 us)
Async XLA Ops:
  0.6 29.5 %collective-permute-start = (bf16[2,8,2,512]{3,2,1,0:T(2,128)(2,1)}, bf16[2,8,2,512]{3,2,1,0:T(2,128)(2,1)S(1)}, u32[]{:S(2)}, u32[]{:S(2)}) collective-permute-start(bf16[2,8,2,512]{3,2,1,0:T(2,128)(2,1)} %param.6), channel_id=1, source_target_pairs={{1,0},{3,2},{5,4},{7,6},{9,8},{11,10},{13,12},{15,14},{17,16},{19,... | collective-permute-start | bytes 98312 | tf_op jit(solution)/shard_map/ppermute | solution.py:16
  1.9 0.7 %copy-start.4 = (s32[2]{0:T(128)S(1)}, s32[2]{0:T(128)}, u32[]{:S(2)}) copy-start(s32[2]{0:T(128)} %param.11) | copy-start | bytes 28
  2.6 0.7 %copy-start.3 = (bf16[2,128]{1,0:T(2,128)(2,1)S(1)}, bf16[2,128]{1,0:T(2,128)(2,1)}, u32[]{:S(2)}) copy-start(bf16[2,128]{1,0:T(2,128)(2,1)} %param.7) | copy-start | bytes 1540
  26.3 0.7 %copy-start.1 = (s32[2]{0:T(128)S(1)}, s32[2]{0:T(128)}, u32[]{:S(2)}) copy-start(s32[2]{0:T(128)} %param.9) | copy-start | bytes 28
  26.3 0.7 %copy-start.2 = (s32[2]{0:T(128)S(1)}, s32[2]{0:T(128)}, u32[]{:S(2)}) copy-start(s32[2]{0:T(128)} %param.8) | copy-start | bytes 28
  29.5 0.8 %copy-start = (bf16[2,8,2,512]{3,2,1,0:T(2,128)(2,1)S(1)}, bf16[2,8,2,512]{3,2,1,0:T(2,128)(2,1)}, u32[]{:S(2)}) copy-start(bf16[2,8,2,512]{3,2,1,0:T(2,128)(2,1)} %param.6) | copy-start | bytes 98308
  36.0 6.2 %copy-start.5 = (s32[2]{0:T(128)S(1)}, s32[2]{0:T(128)}, u32[]{:S(2)}) copy-start(s32[2]{0:T(128)} %param.10) | copy-start | bytes 28
  36.0 6.8 %collective-permute-start.1 = (f32[2,8,104]{2,1,0:T(8,128)S(1)}, f32[2,8,104]{2,1,0:T(8,128)S(1)}, u32[]{:S(2)}, u32[]{:S(2)}) collective-permute-start(f32[2,8,104]{2,1,0:T(8,128)S(1)} %get-tuple-element.67), channel_id=1, source_target_pairs={{0,1},{2,3},{4,5},{6,7},{8,9},{10,11},{12,13},{14,15},{16,17},{18,... | collective-permute-start | bytes 19976 | tf_op jit(solution)/shard_map/ppermute | solution.py:27
  40.7 5.5 %collective-permute-start.2 = (f32[2,8,104]{2,1,0:T(8,128)S(1)}, f32[2,8,104]{2,1,0:T(8,128)S(1)}, u32[]{:S(2)}, u32[]{:S(2)}) collective-permute-start(f32[2,8,104]{2,1,0:T(8,128)S(1)} %get-tuple-element.68), channel_id=1, source_target_pairs={{1,0},{3,2},{5,4},{7,6},{9,8},{11,10},{13,12},{15,14},{17,16},{19,... | collective-permute-start | bytes 19976 | tf_op jit(solution)/shard_map/ppermute | solution.py:29
where the time goes:
time: 62.8 us; the launch traced here: 62.5 us
  blocking collectives  23.1 us (37%)
  local copies, waits for them, and re-layouts  21.7 us (35%)
  starting transfers between devices  7.43 us (12%)
  other arithmetic  4.6 us (7%)
  waiting for transfers between devices  3.4 us (5%)
  matrix products  1.32 us (2%)
  between operations  0.91 us (1%)
    all_gather x1, blocking collectives, body(): whole = lax.all_gather(replica, ('beam', 'pulse'), axis=1, tiled=True)  23.1 us
    gather x8, local copies, waits for them, and re-layouts, window(): return lax.dynamic_slice_in_dim(block, start, length, 1)  11.1 us
    ppermute x1, starting transfers between devices, padded_2(): lax.ppermute(tail, axis, [(i, (i + 1) % count) for i in range(ends)])  4.67 us
    gather x8, local copies, waits for them, and re-layouts  3.94 us
    another operation x4, other arithmetic  3.57 us
    ppermute x1, waiting for transfers between devices, padded_2(): lax.ppermute(head, axis, [((i + 1) % count, i) for i in range(ends)])  3.4 us
    unnamed x16, local copies, waits for them, and re-layouts  3.09 us
    another operation x4, local copies, waits for them, and re-layouts, skewed(): flat = jnp.tile(padded, TILE)[:TILE * width]  1.53 us
  transfers between devices with their start and end apart: 3, of which 1 were waited for; matrix products, arithmetic and copies ran while one was open for 6% of the time, Pallas kernels for 0%

commit v1 on v0

--- a/solution.py
+++ b/solution.py
@@ -118,7 +118,12 @@
 
 
 def body(signal, replica, guard_cells, train_cells, scale_index, offsets):
-    whole = lax.all_gather(replica, ("beam", "pulse"), axis=1, tiled=True)
+    whole = jnp.concatenate(
+        lax.all_to_all(
+            jnp.stack([replica] * lax.axis_size(("beam", "pulse"))), ("beam", "pulse"), 0, 0
+        ),
+        axis=1,
+    )
     panel_real, panel_imag = panels(whole)
     gate_count = signal.shape[3]
     margin = GUARD_MAX + TRAIN_MAX

time: 62.8 us -> 50.3 us (0.80)
  blocking collectives: 23.1 us -> 0 us
  starting transfers between devices: 7.43 us -> 13.7 us
  waiting for transfers between devices: 3.4 us -> 6.91 us
  local copies, waits for them, and re-layouts: 21.7 us -> 22.4 us
    all_gather x1 -> x0, blocking collectives: 23.1 us -> none  [body(): whole = lax.all_gather(replica, ('beam', 'pulse'), axis=1, tiled=True)]
    all_to_all x0 -> x1, starting transfers between devices: none -> 7.39 us  [body(): lax.all_to_all(jnp.stack([replica] * lax.axis_size(('beam', 'pulse'))), (...]
    all_to_all x0 -> x1, waiting for transfers between devices: none -> 3.5 us  [body(): lax.all_to_all(jnp.stack([replica] * lax.axis_size(('beam', 'pulse'))), (...]
    another operation x4 -> x5, local copies, waits for them, and re-layouts: 0.22 us -> 1.48 us  [the longest x1 1.26 us: body(): jnp.stack([replica] * lax.axis_size(('beam', 'pulse')))]
    ppermute x1, starting transfers between devices: 4.67 us -> 3.55 us  [padded_2(): lax.ppermute(tail, axis, [(i, (i + 1) % count) for i in range(ends)])]
    unnamed x16 -> x14, local copies, waits for them, and re-layouts: 3.09 us -> 2.49 us
  transfers between devices with their start and end apart: 3 -> 4, of which waited for: 1 -> 2; matrix products, arithmetic and copies ran while one was open for 6% -> 7% of each run, Pallas kernels for 0% -> 0%
where the time goes in v1:
time: 50.3 us; the launch traced here: 49.9 us
  local copies, waits for them, and re-layouts  22.4 us (45%)
  starting transfers between devices  13.7 us (27%)
  waiting for transfers between devices  6.91 us (14%)
  other arithmetic  4.6 us (9%)
  matrix products  1.32 us (3%)
  between operations  0.92 us (2%)
    gather x8, local copies, waits for them, and re-layouts, window(): return lax.dynamic_slice_in_dim(block, start, length, 1)  11.1 us
    all_to_all x1, starting transfers between devices, body(): lax.all_to_all(jnp.stack([replica] * lax.axis_size(('beam', 'pulse'))), (...  7.39 us
    gather x8, local copies, waits for them, and re-layouts  4.09 us
    another operation x4, other arithmetic  3.57 us
    ppermute x1, starting transfers between devices, padded_2(): lax.ppermute(tail, axis, [(i, (i + 1) % count) for i in range(ends)])  3.55 us
    all_to_all x1, waiting for transfers between devices, body(): lax.all_to_all(jnp.stack([replica] * lax.axis_size(('beam', 'pulse'))), (...  3.5 us
    ppermute x1, waiting for transfers between devices, padded_2(): lax.ppermute(head, axis, [((i + 1) % count, i) for i in range(ends)])  3.4 us
    unnamed x14, local copies, waits for them, and re-layouts  2.49 us
  transfers between devices with their start and end apart: 4, of which 2 were waited for; matrix products, arithmetic and copies ran while one was open for 7% of the time, Pallas kernels for 0%

profile of v1, /device:TPU:0, one launch (start us, length us, event | category | flops | bytes accessed | tf_op | source)
XLA Modules:
  0.0 49.9 jit_solution(46706849598493653)
XLA Ops:
  0.6 1.3 %stack.56 = bf16[16,2,128]{2,1,0:T(2,128)(2,1)} broadcast(bf16[2,128]{1,0:T(2,128)(2,1)} %param.7), dimensions={1,2} | broadcast | bytes 8704 | tf_op jit(solution)/shard_map/stack | solution.py:123
  1.9 7.4 %all-to-all-start = ((bf16[16,2,128]{2,1,0:T(2,128)(2,1)}), bf16[16,2,128]{2,1,0:T(2,128)(2,1)S(1)}, u32[]{:S(2)}, u32[]{:S(2)}) async-start(bf16[16,2,128]{2,1,0:T(2,128)(2,1)} %stack.56), calls=%async_computation | async-start | bytes 16384 | tf_op jit(solution)/shard_map/all_to_all | solution.py:122
  9.3 1.3 %collective-permute-start = (bf16[2,8,2,512]{3,2,1,0:T(2,128)(2,1)}, bf16[2,8,2,512]{3,2,1,0:T(2,128)(2,1)S(1)}, u32[]{:S(2)}, u32[]{:S(2)}) collective-permute-start(bf16[2,8,2,512]{3,2,1,0:T(2,128)(2,1)} %param.6), channel_id=1, source_target_pairs={{1,0},{3,2},{5,4},{7,6},{9,8},{11,10},{13,12},{15,14},{17,16},{19,... | collective-permute-start | bytes 98312 | tf_op jit(solution)/shard_map/ppermute | solution.py:16
  10.6 0.0 copy-start.3
  10.6 0.6 %copy-done.3 = s32[2]{0:T(128)S(1)} copy-done((s32[2]{0:T(128)S(1)}, s32[2]{0:T(128)}, u32[]{:S(2)}) %copy-start.3) | copy-done | bytes 32
  11.2 0.0 copy-start.1
  11.2 0.0 copy-start.2
  11.3 0.6 %copy-done.1 = s32[2]{0:T(128)S(1)} copy-done((s32[2]{0:T(128)S(1)}, s32[2]{0:T(128)}, u32[]{:S(2)}) %copy-start.1) | copy-done | bytes 32
  11.9 0.0 copy-done.2
  11.9 0.1 add_convert_fusion
  12.0 0.1 copy.42
  12.1 3.5 %all-to-all-done = bf16[16,2,128]{2,1,0:T(2,128)(2,1)S(1)} async-done(((bf16[16,2,128]{2,1,0:T(2,128)(2,1)}), bf16[16,2,128]{2,1,0:T(2,128)(2,1)S(1)}, u32[]{:S(2)}, u32[]{:S(2)}) %all-to-all-start) | async-done | bytes 8224 | tf_op jit(solution)/shard_map/all_to_all | solution.py:122
  15.7 0.7 %tile.9 = bf16[278656]{0:T(1024)(128)(2,1)S(1)} reshape(bf16[128,2177]{1,0:T(8,128)(2,1)S(1)} %tile.8) | data formatting | bytes 1114624 | tf_op jit(solution)/shard_map/tile | solution.py:41
  16.5 0.6 %reshape.130 = bf16[128,2176]{1,0:T(8,128)(2,1)S(1)} reshape(bf16[278528]{0:T(1024)(128)(2,1)S(1)} %slice.100) | data formatting | bytes 1114112 | tf_op jit(solution)/shard_map/reshape | solution.py:42
  17.2 0.7 %tile.21 = bf16[278656]{0:T(1024)(128)(2,1)S(1)} reshape(bf16[128,2177]{1,0:T(8,128)(2,1)S(1)} %tile.20) | data formatting | bytes 1114624 | tf_op jit(solution)/shard_map/tile | solution.py:41
  17.9 0.0 copy-start
  17.9 0.6 %reshape.131 = bf16[128,2176]{1,0:T(8,128)(2,1)S(1)} reshape(bf16[278528]{0:T(1024)(128)(2,1)S(1)} %slice.103) | data formatting | bytes 1114112 | tf_op jit(solution)/shard_map/reshape | solution.py:42
  18.6 0.0 collective-permute-done
  18.6 0.1 copy-done
  18.7 0.1 fusion.4
  18.8 4.2 %while.1 = (s32[]{:T(128)}, bf16[2,8,2,2688]{3,2,1,0:T(2,128)(2,1)S(1)}, s32[2,4]{1,0:T(2,128)S(1)}, bf16[2,8,2,2560]{3,1,0,2:T(8,128)(2,1)S(1)}, s32[]{:T(128)}) while((s32[]{:T(128)}, bf16[2,8,2,2688]{3,2,1,0:T(2,128)(2,1)S(1)}, s32[2,4]{1,0:T(2,128)S(1)}, bf16[2,8,2,2560]{3,1,0,2:T(8,128)(2,1)S(1)}, s32[]{:T(128)}) %tuple.43), condition=%wide.while_cond, body=%wide.while_body.sunk | while | flops 2 | bytes 327813 | solution.py:53
  18.8 0.6 %fusion.34 = (s32[1,1]{1,0:T(1,128)}, s32[1,1]{1,0:T(1,128)}) fusion(s32[1,4]{1,0:T(1,128)S(1)} %constant_dynamic-slice_fusion.4), kind=kLoop, calls=%fused_computation.60.clone.1 | loop fusion | bytes 16 | tf_op jit(solution)/shard_map/vmap()/gather
  19.4 1.4 %constant_dynamic-slice_fusion.5 = bf16[1,8,2,2560]{3,2,1,0:T(2,128)(2,1)S(1)} fusion(bf16[2,8,2,2688]{3,2,1,0:T(2,128)(2,1)S(1)} %get-tuple-element.115, s32[]{:T(128)} %bitcast.75, s32[]{:T(128)} %bitcast.76), kind=kLoop, calls=%fused_computation.6.clone.1 | loop fusion | bytes 163848 | tf_op jit(solution)/shard_map/vmap()/gather
  20.9 0.6 %fusion.34 = (s32[1,1]{1,0:T(1,128)}, s32[1,1]{1,0:T(1,128)}) fusion(s32[1,4]{1,0:T(1,128)S(1)} %constant_dynamic-slice_fusion.4), kind=kLoop, calls=%fused_computation.60.clone.1 | loop fusion | bytes 16 | tf_op jit(solution)/shard_map/vmap()/gather
  21.5 1.4 %constant_dynamic-slice_fusion.5 = bf16[1,8,2,2560]{3,2,1,0:T(2,128)(2,1)S(1)} fusion(bf16[2,8,2,2688]{3,2,1,0:T(2,128)(2,1)S(1)} %get-tuple-element.115, s32[]{:T(128)} %bitcast.75, s32[]{:T(128)} %bitcast.76), kind=kLoop, calls=%fused_computation.6.clone.1 | loop fusion | bytes 163848 | tf_op jit(solution)/shard_map/vmap()/gather
  23.0 0.1 pad_maximum_fusion
  23.2 0.3 fusion.24
  23.5 0.3 fusion.23
  23.8 0.3 fusion.1
  24.2 0.3 fusion
  24.5 0.1 fusion.22
  24.6 0.0 copy-start.4
  24.6 3.5 %collective-permute-start.1 = (f32[2,8,104]{2,1,0:T(8,128)S(1)}, f32[2,8,104]{2,1,0:T(8,128)S(1)}, u32[]{:S(2)}, u32[]{:S(2)}) collective-permute-start(f32[2,8,104]{2,1,0:T(8,128)S(1)} %get-tuple-element.65), channel_id=1, source_target_pairs={{0,1},{2,3},{4,5},{6,7},{8,9},{10,11},{12,13},{14,15},{16,17},{18,... | collective-permute-start | bytes 19976 | tf_op jit(solution)/shard_map/ppermute | solution.py:27
  28.1 1.5 %collective-permute-start.2 = (f32[2,8,104]{2,1,0:T(8,128)S(1)}, f32[2,8,104]{2,1,0:T(8,128)S(1)}, u32[]{:S(2)}, u32[]{:S(2)}) collective-permute-start(f32[2,8,104]{2,1,0:T(8,128)S(1)} %get-tuple-element.66), channel_id=1, source_target_pairs={{1,0},{3,2},{5,4},{7,6},{9,8},{11,10},{13,12},{15,14},{17,16},{19,... | collective-permute-start | bytes 19976 | tf_op jit(solution)/shard_map/ppermute | solution.py:29
  29.6 0.0 copy-done.4
  29.7 0.6 %copy.57 = bf16[2,8,2,512]{3,2,1,0:T(2,128)(2,1)} copy(bf16[2,8,2,512]{3,1,2,0:T(8,128)(2,1)S(1)} %copy_bitcast_fusion) | data formatting | bytes 65536
  30.3 0.0 collective-permute-done.1
  30.3 3.4 %collective-permute-done.2 = f32[2,8,104]{2,1,0:T(8,128)S(1)} collective-permute-done((f32[2,8,104]{2,1,0:T(8,128)S(1)}, f32[2,8,104]{2,1,0:T(8,128)S(1)}, u32[]{:S(2)}, u32[]{:S(2)}) %collective-permute-start.2) | collective-permute-done | bytes 6688 | tf_op jit(solution)/shard_map/ppermute | solution.py:29
  33.7 0.1 fusion.5
  33.8 3.4 %reduce-window.6 = f32[2,8,6,128]{3,1,2,0:T(8,128)S(1)} reduce-window(f32[2,8,6,128]{3,1,2,0:T(8,128)S(1)} %fusion.5, f32[]{:T(128)} %constant.72.clone.1), window={size=1x1x1x128 pad=0_0x0_0x0_0x127_0}, to_apply=%region_0.1 | reduce-window | flops 1560576 | bytes 98308 | tf_op jit(solution)/shard_map/reduce-window
  37.2 0.1 slice.108
  37.3 0.1 copy.50
  37.4 0.1 add_bitcast_fusion
  37.5 0.3 copy.61
  37.8 0.3 concatenate.37
  38.1 2.6 %gather_fusion.3 = f32[2,8,512]{1,0,2:T(2,128)S(1)} fusion(f32[2,8,721]{1,0,2:T(2,128)S(1)} %concatenate.37, s32[2]{0:T(128)S(1)} %get-tuple-element.72), kind=kCustom, calls=%fused_computation.3 | custom fusion | bytes 65560 | tf_op jit(solution)/shard_map/vmap()/gather | solution.py:103
  40.7 0.2 copy.56
  40.9 2.6 %gather_fusion.2 = f32[2,8,512]{1,0,2:T(2,128)S(1)} fusion(f32[2,8,721]{1,0,2:T(2,128)S(1)} %concatenate.37, s32[2]{0:T(128)S(1)} %get-tuple-element.70), kind=kCustom, calls=%fused_computation.2 | custom fusion | bytes 65560 | tf_op jit(solution)/shard_map/vmap()/gather | solution.py:103
  43.5 0.2 copy.55
  43.7 2.6 %gather_fusion.1 = f32[2,8,512]{1,0,2:T(2,128)S(1)} fusion(f32[2,8,721]{1,0,2:T(2,128)S(1)} %concatenate.37, s32[2]{0:T(128)S(1)} %get-tuple-element.69), kind=kCustom, calls=%fused_computation.1 | custom fusion | bytes 65560 | tf_op jit(solution)/shard_map/vmap()/gather | solution.py:103
  46.3 0.2 copy.54
  46.4 2.6 %gather_fusion = f32[2,8,512]{1,0,2:T(2,128)S(1)} fusion(f32[2,8,721]{1,0,2:T(2,128)S(1)} %concatenate.37, s32[2]{0:T(128)S(1)} %get-tuple-element.71), kind=kCustom, calls=%fused_computation | custom fusion | bytes 65560 | tf_op jit(solution)/shard_map/vmap()/gather | solution.py:103
  49.1 0.2 copy.53
  49.2 0.7 %multiply_divide_fusion = f32[2,8,512]{2,1,0:T(8,128)} fusion(f32[2,8,512]{2,1,0:T(8,128)S(1)} %copy.55, f32[2,8,512]{2,1,0:T(8,128)S(1)} %copy.56, f32[2,8,512]{2,1,0:T(8,128)S(1)} %copy.53, f32[2,8,512]{2,1,0:T(8,128)S(1)} %copy.54, f32[2,512]{1,0:T(2,128)S(1)} %add_convert_fusion, f32[2]{0:T(128)S(1)} %multiply_exponential_fusion, ...), kind=kLoop, calls=%fused_computation.27 | loop fusion | flops 98304 | bytes 200712 | tf_op jit(solution)/shard_map/div | solution.py:117
  (26 shorter events, 0.4 us)
Async XLA Ops:
  1.9 13.8 %all-to-all-start = ((bf16[16,2,128]{2,1,0:T(2,128)(2,1)}), bf16[16,2,128]{2,1,0:T(2,128)(2,1)S(1)}, u32[]{:S(2)}, u32[]{:S(2)}) async-start(bf16[16,2,128]{2,1,0:T(2,128)(2,1)} %stack.56), calls=%async_computation | async-start | bytes 16384 | tf_op jit(solution)/shard_map/all_to_all | solution.py:122
  9.3 9.3 %collective-permute-start = (bf16[2,8,2,512]{3,2,1,0:T(2,128)(2,1)}, bf16[2,8,2,512]{3,2,1,0:T(2,128)(2,1)S(1)}, u32[]{:S(2)}, u32[]{:S(2)}) collective-permute-start(bf16[2,8,2,512]{3,2,1,0:T(2,128)(2,1)} %param.6), channel_id=1, source_target_pairs={{1,0},{3,2},{5,4},{7,6},{9,8},{11,10},{13,12},{15,14},{17,16},{19,... | collective-permute-start | bytes 98312 | tf_op jit(solution)/shard_map/ppermute | solution.py:16
  10.6 0.7 %copy-start.3 = (s32[2]{0:T(128)S(1)}, s32[2]{0:T(128)}, u32[]{:S(2)}) copy-start(s32[2]{0:T(128)} %param.11) | copy-start | bytes 28
  11.2 0.7 %copy-start.1 = (s32[2]{0:T(128)S(1)}, s32[2]{0:T(128)}, u32[]{:S(2)}) copy-start(s32[2]{0:T(128)} %param.9) | copy-start | bytes 28
  11.2 0.7 %copy-start.2 = (s32[2]{0:T(128)S(1)}, s32[2]{0:T(128)}, u32[]{:S(2)}) copy-start(s32[2]{0:T(128)} %param.8) | copy-start | bytes 28
  17.9 0.8 %copy-start = (bf16[2,8,2,512]{3,2,1,0:T(2,128)(2,1)S(1)}, bf16[2,8,2,512]{3,2,1,0:T(2,128)(2,1)}, u32[]{:S(2)}) copy-start(bf16[2,8,2,512]{3,2,1,0:T(2,128)(2,1)} %param.6) | copy-start | bytes 98308
  24.6 5.0 %copy-start.4 = (s32[2]{0:T(128)S(1)}, s32[2]{0:T(128)}, u32[]{:S(2)}) copy-start(s32[2]{0:T(128)} %param.10) | copy-start | bytes 28
  24.6 5.7 %collective-permute-start.1 = (f32[2,8,104]{2,1,0:T(8,128)S(1)}, f32[2,8,104]{2,1,0:T(8,128)S(1)}, u32[]{:S(2)}, u32[]{:S(2)}) collective-permute-start(f32[2,8,104]{2,1,0:T(8,128)S(1)} %get-tuple-element.65), channel_id=1, source_target_pairs={{0,1},{2,3},{4,5},{6,7},{8,9},{10,11},{12,13},{14,15},{16,17},{18,... | collective-permute-start | bytes 19976 | tf_op jit(solution)/shard_map/ppermute | solution.py:27
  28.1 5.5 %collective-permute-start.2 = (f32[2,8,104]{2,1,0:T(8,128)S(1)}, f32[2,8,104]{2,1,0:T(8,128)S(1)}, u32[]{:S(2)}, u32[]{:S(2)}) collective-permute-start(f32[2,8,104]{2,1,0:T(8,128)S(1)} %get-tuple-element.66), channel_id=1, source_target_pairs={{1,0},{3,2},{5,4},{7,6},{9,8},{11,10},{13,12},{15,14},{17,16},{19,... | collective-permute-start | bytes 19976 | tf_op jit(solution)/shard_map/ppermute | solution.py:29
